TPU v7x, 512 devices: a whole 4x8x8 slice. The times are simulated.
512 devices in a mesh: die: 32 (over x, y), ty: 4 (over z_lo), tx: 4 (over z_hi, core).
Axes of the slice: x: 4, y: 8, z: 8 (z_hi: 2, z_lo: 4; z = z_hi * 4 + z_lo), core: 2. Of those that a mesh axis runs over, the one named last changes fastest.
Arguments:
- raster: float32 [32, 1024, 4096], P('die', 'ty', 'tx'), may hold values from -12 to 12
- shift_pick: int32 [32, 4, 4], P('die', 'ty', 'tx'), may hold values from 0 to 7
- offsets: int32 [32, 4, 4, 2], P('die', 'ty', 'tx'), may hold values from -5 to 4
Outputs:
- next_map: float32 [32, 1024, 4096], P('die', 'ty', 'tx')
- prev_map: float32 [32, 1024, 4096], P('die', 'ty', 'tx')
All inputs are finite; a program needn't handle non-finite values.
Results may differ from a plain program's by a relative error of at most 0.0003.
Values sent between devices are 32-bit elements; how exact they have to be, the bound alone decides.
A program may use at most 64 MiB of HBM per device.

v0:
```python
import jax
import jax.numpy as jnp
from jax import lax
from jax.sharding import PartitionSpec as P

TH = 256
TW = 1024
R = 4
RG = 6
HW = 11


def extended(block, sides, width):
    for axis, dim in sides:
        count = lax.axis_size(axis)
        forward = [(i, i + 1) for i in range(count - 1)]
        backward = [(target, source) for source, target in forward]
        low = lax.ppermute(
            lax.slice_in_dim(block, block.shape[dim] - width, None, axis=dim), axis, forward
        )
        high = lax.ppermute(lax.slice_in_dim(block, 0, width, axis=dim), axis, backward)
        block = jnp.concatenate([low, block, high], axis=dim)
    return block


def shifted(block, axis, distance):
    devices = range(lax.axis_size(axis))
    route = [(i - distance, i) for i in devices if i - distance in devices]
    return lax.ppermute(block, axis, route)


def gauss_taps(sigma):
    spots = jnp.arange(-RG, RG + 1).astype(jnp.float32)
    raw = jnp.exp(-spots * spots / (2.0 * sigma * sigma))
    return raw / jnp.sum(raw)


def blur_tile(image, sigma):
    taps = gauss_taps(sigma)
    column_sum = taps[0] * image[0:TH, :]
    for shift in range(1, 2 * RG + 1):
        column_sum = column_sum + taps[shift] * image[shift : shift + TH, :]
    total = taps[0] * column_sum[:, 0:TW]
    for shift in range(1, 2 * RG + 1):
        total = total + taps[shift] * column_sum[:, shift : shift + TW]
    return total


def tile_dog(block, row_off, col_off, pick):
    row_start = row_off + R + 1
    col_start = col_off + R + 1
    window = lax.dynamic_slice(block, (row_start, col_start), (TH + 2 * RG + 1, TW + 2 * RG + 1))
    frac_y = (pick % 4).astype(jnp.float32) * 0.25 + 0.125
    frac_x = (pick // 4).astype(jnp.float32) * 0.5 + 0.25
    upper = (1.0 - frac_x) * window[:-1, :-1] + frac_x * window[:-1, 1:]
    lower = (1.0 - frac_x) * window[1:, :-1] + frac_x * window[1:, 1:]
    aligned = (1.0 - frac_y) * upper + frac_y * lower
    return blur_tile(aligned, 1.0) - blur_tile(aligned, 2.0)


def body(raster, shift_pick, offsets):
    tile = raster[0]
    block = extended(tile, (("ty", 0), ("tx", 1)), HW)
    dog = tile_dog(block, offsets[0, 0, 0, 0], offsets[0, 0, 0, 1], shift_pick[0, 0, 0])
    position = lax.axis_index("die")
    last_die = lax.axis_size("die") - 1
    following = shifted(dog, "die", -1)
    next_map = jnp.where(position < last_die, following - dog, jnp.zeros_like(dog))
    prev_map = shifted(next_map, "die", 1)
    return (next_map[None], prev_map[None])


def solution(mesh):
    in_specs = (P("die", "ty", "tx"), P("die", "ty", "tx"), P("die", "ty", "tx", None))
    out_specs = (P("die", "ty", "tx"), P("die", "ty", "tx"))
    return jax.shard_map(body, mesh=mesh, in_specs=in_specs, out_specs=out_specs, check_vma=False)
```

profile of v0, /device:TPU:7, one launch (start us, length us, event | category | flops | bytes accessed | tf_op | source)
XLA Modules:
  0.0 124.7 jit_solution(17035672430455421143)
XLA Ops:
  0.6 0.9 slice_bitcast_fusion.1
  1.5 4.0 %collective-permute-start = (f32[11,1024]{1,0:T(8,128)S(1)}, f32[11,1024]{1,0:T(8,128)S(1)}, u32[]{:S(2)}, u32[]{:S(2)}) collective-permute-start(f32[11,1024]{1,0:T(8,128)S(1)} %get-tuple-element.4), channel_id=1, source_target_pairs={{0,4},{4,8},{8,12},{1,5},{5,9},{9,13},{2,6},{6,10},{10,14},{3,7},{... | collective-permute-start | bytes 135176 | tf_op jit(solution)/shard_map/ppermute | solution.py:18
  5.5 1.3 %collective-permute-start.1 = (f32[11,1024]{1,0:T(8,128)S(1)}, f32[11,1024]{1,0:T(8,128)S(1)}, u32[]{:S(2)}, u32[]{:S(2)}) collective-permute-start(f32[11,1024]{1,0:T(8,128)S(1)} %get-tuple-element.5), channel_id=1, source_target_pairs={{4,0},{8,4},{12,8},{5,1},{9,5},{13,9},{6,2},{10,6},{14,10},{7,3},{... | collective-permute-start | bytes 135176 | tf_op jit(solution)/shard_map/ppermute | solution.py:21
  6.8 0.6 fusion.30
  7.4 0.6 fusion.31
  8.1 0.7 broadcast_divide_fusion.1
  8.7 0.7 fusion.33
  9.4 0.7 broadcast_divide_fusion
  10.1 0.7 fusion.34
  11.2 1.4 %pad_maximum_fusion = f32[278,1024]{1,0:T(8,128)S(1)} fusion(f32[11,1024]{1,0:T(8,128)S(1)} %collective-permute-done.1, f32[256,1024]{1,0:T(8,128)} %bitcast.42, f32[11,1024]{1,0:T(8,128)S(1)} %collective-permute-done), kind=kLoop, calls=%fused_computation.11 | loop fusion | flops 569344 | bytes 2277376 | tf_op jit(solution)/shard_map/concatenate | solution.py:22
  12.6 11.1 %collective-permute-start.2 = (f32[278,11]{1,0:T(8,128)S(1)}, f32[278,11]{1,0:T(8,128)S(1)}, u32[]{:S(2)}, u32[]{:S(2)}) collective-permute-start(f32[278,11]{1,0:T(8,128)S(1)} %get-tuple-element.3), channel_id=1, source_target_pairs={{0,1},{1,2},{2,3},{4,5},{5,6},{6,7},{8,9},{9,10},{10,11},{12,13},{... | collective-permute-start | bytes 36704 | tf_op jit(solution)/shard_map/ppermute | solution.py:18
  23.7 1.9 %collective-permute-start.3 = (f32[278,11]{1,0:T(8,128)S(1)}, f32[278,11]{1,0:T(8,128)S(1)}, u32[]{:S(2)}, u32[]{:S(2)}) collective-permute-start(f32[278,11]{1,0:T(8,128)S(1)} %get-tuple-element.2), channel_id=1, source_target_pairs={{1,0},{2,1},{3,2},{5,4},{6,5},{7,6},{9,8},{10,9},{11,10},{13,12},{... | collective-permute-start | bytes 36704 | tf_op jit(solution)/shard_map/ppermute | solution.py:21
  25.7 0.6 fusion.35
  29.5 4.9 %collective-permute-done.3 = f32[278,11]{1,0:T(8,128)S(1)} collective-permute-done((f32[278,11]{1,0:T(8,128)S(1)}, f32[278,11]{1,0:T(8,128)S(1)}, u32[]{:S(2)}, u32[]{:S(2)}) %collective-permute-start.3) | collective-permute-done | bytes 12264 | tf_op jit(solution)/shard_map/ppermute | solution.py:21
  34.5 1.0 concatenate.7
  35.4 1.4 %fusion.2 = f32[268,1036]{1,0:T(8,128)S(1)} fusion(f32[278,1046]{1,0:T(8,128)S(1)} %concatenate.7, s32[]{:T(128)S(6)} %add.272, s32[]{:T(128)S(6)} %add.271, s32[]{:T(128)S(6)} %select_n.29, s32[]{:T(128)S(6)} %select_n.28, f32[]{:T(128)S(6)} %add.210, f32[]{:T(128)S(6)} %add.211, f32[]{:T(128)S(6)} %sub.19, f32[]{:T(128)S(6)} %sub.17), kind=kLoop, calls=%fused_computation.3 | loop fusion | flops 2498832 | bytes 5552992 | tf_op jit(solution)/shard_map/add | solution.py:57
  36.8 9.7 %multiply_add_fusion.1 = f32[256,1036]{1,0:T(8,128)S(1)} fusion(f32[268,1036]{1,0:T(8,128)S(1)} %fusion.2, f32[]{:T(128)} %bitcast.20, f32[]{:T(128)} %bitcast.19, f32[]{:T(128)} %bitcast.18, f32[]{:T(128)} %bitcast.17, f32[]{:T(128)} %bitcast.16, f32[]{:T(128)} %bitcast.15, f32[]{:T(128)} %bitcast.14, f32[]{:T(128)} %bitcast.13, f32[]{:T(128)} %bitcast.12, ...), kind=kLoop, calls=%fused_computation.10 | loop fusion | flops 6630400 | bytes 14852148 | tf_op jit(solution)/shard_map/add | solution.py:42
  46.5 9.6 %multiply_add_fusion = f32[256,1036]{1,0:T(8,128)S(1)} fusion(f32[268,1036]{1,0:T(8,128)S(1)} %fusion.2, f32[]{:T(128)} %bitcast.33, f32[]{:T(128)} %bitcast.32, f32[]{:T(128)} %bitcast.31, f32[]{:T(128)} %bitcast.30, f32[]{:T(128)} %bitcast.29, f32[]{:T(128)} %bitcast.28, f32[]{:T(128)} %bitcast.27, f32[]{:T(128)} %bitcast.26, f32[]{:T(128)} %bitcast.25, ...), kind=kLoop, calls=%fused_computation.9 | loop fusion | flops 6630400 | bytes 14852148 | tf_op jit(solution)/shard_map/add | solution.py:42
  56.1 22.9 %fusion.6 = f32[256,1024]{1,0:T(8,128)S(1)} fusion(f32[256,1036]{1,0:T(8,128)S(1)} %multiply_add_fusion, f32[256,1036]{1,0:T(8,128)S(1)} %multiply_add_fusion.1, f32[]{:T(128)} %bitcast.33, f32[]{:T(128)} %bitcast.32, f32[]{:T(128)} %bitcast.31, f32[]{:T(128)} %bitcast.30, f32[]{:T(128)} %bitcast.29, f32[]{:T(128)} %bitcast.28, f32[]{:T(128)} %bitcast.27, ...), kind=kLoop, calls=%fused_computation.14 | loop fusion | flops 13369344 | bytes 28311656 | tf_op jit(solution)/shard_map/sub | solution.py:58
  79.0 5.4 %collective-permute-start.4 = (f32[256,1024]{1,0:T(8,128)S(1)}, f32[256,1024]{1,0:T(8,128)S(1)}, u32[]{:S(2)}, u32[]{:S(2)}) collective-permute-start(f32[256,1024]{1,0:T(8,128)S(1)} %fusion.6), channel_id=1, source_target_pairs={{16,0},{32,16},{48,32},{64,48},{80,64},{96,80},{112,96},{128,112},... | collective-permute-start | bytes 3145736 | tf_op jit(solution)/shard_map/ppermute | solution.py:29
  84.4 15.9 %collective-permute-done.4 = f32[256,1024]{1,0:T(8,128)S(1)} collective-permute-done((f32[256,1024]{1,0:T(8,128)S(1)}, f32[256,1024]{1,0:T(8,128)S(1)}, u32[]{:S(2)}, u32[]{:S(2)}) %collective-permute-start.4) | collective-permute-done | bytes 1048608 | tf_op jit(solution)/shard_map/ppermute | solution.py:29
  100.6 2.0 %collective-permute-start.5 = (f32[256,1024]{1,0:T(8,128)S(1)}, f32[256,1024]{1,0:T(8,128)S(1)}, u32[]{:S(2)}, u32[]{:S(2)}) collective-permute-start(f32[256,1024]{1,0:T(8,128)S(1)} %subtract_select_fusion), channel_id=1, source_target_pairs={{0,16},{16,32},{32,48},{48,64},{64,80},{80,96},{96,112},{112,128},... | collective-permute-start | bytes 3145736 | tf_op jit(solution)/shard_map/ppermute | solution.py:29
  102.6 21.2 %collective-permute-done.5 = f32[256,1024]{1,0:T(8,128)S(1)} collective-permute-done((f32[256,1024]{1,0:T(8,128)S(1)}, f32[256,1024]{1,0:T(8,128)S(1)}, u32[]{:S(2)}, u32[]{:S(2)}) %collective-permute-start.5) | collective-permute-done | bytes 1048608 | tf_op jit(solution)/shard_map/ppermute | solution.py:29
  123.7 1.0 copy.7
  (9 shorter events, 0.7 us)
Async XLA Ops:
  1.5 9.3 %collective-permute-start = (f32[11,1024]{1,0:T(8,128)S(1)}, f32[11,1024]{1,0:T(8,128)S(1)}, u32[]{:S(2)}, u32[]{:S(2)}) collective-permute-start(f32[11,1024]{1,0:T(8,128)S(1)} %get-tuple-element.4), channel_id=1, source_target_pairs={{0,4},{4,8},{8,12},{1,5},{5,9},{9,13},{2,6},{6,10},{10,14},{3,7},{... | collective-permute-start | bytes 135176 | tf_op jit(solution)/shard_map/ppermute | solution.py:18
  5.5 5.6 %collective-permute-start.1 = (f32[11,1024]{1,0:T(8,128)S(1)}, f32[11,1024]{1,0:T(8,128)S(1)}, u32[]{:S(2)}, u32[]{:S(2)}) collective-permute-start(f32[11,1024]{1,0:T(8,128)S(1)} %get-tuple-element.5), channel_id=1, source_target_pairs={{4,0},{8,4},{12,8},{5,1},{9,5},{13,9},{6,2},{10,6},{14,10},{7,3},{... | collective-permute-start | bytes 135176 | tf_op jit(solution)/shard_map/ppermute | solution.py:21
  11.2 14.5 %copy-start.1 = (s32[1,1,1,2]{3,2,1,0:T(1,128)S(1)}, s32[1,1,1,2]{3,2,1,0:T(1,128)}, u32[]{:S(2)}) copy-start(s32[1,1,1,2]{3,2,1,0:T(1,128)} %param.5) | copy-start | bytes 28
  12.6 16.9 %collective-permute-start.2 = (f32[278,11]{1,0:T(8,128)S(1)}, f32[278,11]{1,0:T(8,128)S(1)}, u32[]{:S(2)}, u32[]{:S(2)}) collective-permute-start(f32[278,11]{1,0:T(8,128)S(1)} %get-tuple-element.3), channel_id=1, source_target_pairs={{0,1},{1,2},{2,3},{4,5},{5,6},{6,7},{8,9},{9,10},{10,11},{12,13},{... | collective-permute-start | bytes 36704 | tf_op jit(solution)/shard_map/ppermute | solution.py:18
  23.7 10.7 %collective-permute-start.3 = (f32[278,11]{1,0:T(8,128)S(1)}, f32[278,11]{1,0:T(8,128)S(1)}, u32[]{:S(2)}, u32[]{:S(2)}) collective-permute-start(f32[278,11]{1,0:T(8,128)S(1)} %get-tuple-element.2), channel_id=1, source_target_pairs={{1,0},{2,1},{3,2},{5,4},{6,5},{7,6},{9,8},{10,9},{11,10},{13,12},{... | collective-permute-start | bytes 36704 | tf_op jit(solution)/shard_map/ppermute | solution.py:21
  79.0 21.3 %collective-permute-start.4 = (f32[256,1024]{1,0:T(8,128)S(1)}, f32[256,1024]{1,0:T(8,128)S(1)}, u32[]{:S(2)}, u32[]{:S(2)}) collective-permute-start(f32[256,1024]{1,0:T(8,128)S(1)} %fusion.6), channel_id=1, source_target_pairs={{16,0},{32,16},{48,32},{64,48},{80,64},{96,80},{112,96},{128,112},... | collective-permute-start | bytes 3145736 | tf_op jit(solution)/shard_map/ppermute | solution.py:29
  100.6 24.1 %copy-start = (f32[256,1024]{1,0:T(8,128)}, f32[256,1024]{1,0:T(8,128)S(1)}, u32[]{:S(2)}) copy-start(f32[256,1024]{1,0:T(8,128)S(1)} %subtract_select_fusion) | copy-start | bytes 3145732
  100.6 23.1 %collective-permute-start.5 = (f32[256,1024]{1,0:T(8,128)S(1)}, f32[256,1024]{1,0:T(8,128)S(1)}, u32[]{:S(2)}, u32[]{:S(2)}) collective-permute-start(f32[256,1024]{1,0:T(8,128)S(1)} %subtract_select_fusion), channel_id=1, source_target_pairs={{0,16},{16,32},{32,48},{48,64},{64,80},{80,96},{96,112},{112,128},... | collective-permute-start | bytes 3145736 | tf_op jit(solution)/shard_map/ppermute | solution.py:29
where the time goes:
time: 126 us; the launch traced here: 125 us
  other arithmetic  47.7 us (38%)
  waiting for transfers between devices  42.4 us (34%)
  starting transfers between devices  25.6 us (20%)
  local copies, waits for them, and re-layouts  4.94 us (4%)
  between operations  4.06 us (3%)
    ppermute x2, waiting for transfers between devices, shifted(): return lax.ppermute(block, axis, route)  37.1 us
    sub x1, other arithmetic, tile_dog(): return blur_tile(aligned, 1.0) - blur_tile(aligned, 2.0)  22.9 us
    add x2, other arithmetic, blur_tile(): column_sum = column_sum + taps[shift] * image[shift:shift + TH, :]  19.3 us
    ppermute x2, starting transfers between devices, extended(): lax.ppermute(lax.slice_in_dim(block, block.shape[dim] - width, None, axis...  15.1 us
    ppermute x2, starting transfers between devices, shifted(): return lax.ppermute(block, axis, route)  7.35 us
    ppermute x2, waiting for transfers between devices, extended(): lax.ppermute(lax.slice_in_dim(block, 0, width, axis=dim), axis, backward)  5.29 us
    ppermute x2, starting transfers between devices, extended(): lax.ppermute(lax.slice_in_dim(block, 0, width, axis=dim), axis, backward)  3.21 us
  transfers between devices with their start and end apart: 6, of which 4 were waited for; matrix products, arithmetic and copies ran while one was open for 4% of the time, Pallas kernels for 0%

commit v1 on v0

v1 whole, which is shorter than its diff:
```python
import functools
import math

import jax
import jax.numpy as jnp
from jax import lax
from jax.experimental import pallas as pl
from jax.experimental.pallas import tpu as pltpu
from jax.sharding import PartitionSpec as P

MESH = pl.DeviceIdType.MESH
F32, BF16 = jnp.float32, jnp.bfloat16
TH, TW = 256, 1024
RG = 6
PAD = 16
LANE = 128
CENTER, TOP, BOTTOM = (64, 128), (0, 64), (192, 64)
INNER = ((1, 2), (3, 4), (5, 6))
OUTER = (0, 7)


def tap_weights(step, sigma, frac):
    norm = sum(math.exp(-k * k / (2.0 * sigma * sigma)) for k in range(-RG, RG + 1))

    def gauss(k):
        spot = k.astype(F32)
        value = jnp.exp(spot * spot * (-1.0 / (2.0 * sigma * sigma))) * (1.0 / norm)
        return jnp.where(jnp.abs(k) <= RG, value, 0.0)

    return (1.0 - frac) * gauss(step) + frac * gauss(step - 1)


def split(x):
    high = x.astype(BF16)
    return high, (x - high.astype(F32)).astype(BF16)


def product(ah, al, bh, bl):
    dot = functools.partial(jnp.dot, preferred_element_type=F32)
    return dot(ah, bh) + dot(ah, bl) + dot(al, bh)


def row_matrix(rows, row_off, frac_y):
    span = rows + 2 * PAD
    out = lax.broadcasted_iota(jnp.int32, (rows, span), 0)
    step = lax.broadcasted_iota(jnp.int32, (rows, span), 1) - PAD - out - row_off
    return tap_weights(step, 1.0, frac_y), -tap_weights(step, 2.0, frac_y)


def kernel(pick_ref, off_ref, x_ref, next_ref, prev_ref, pf, ph, plo, wh, wl, ych, ycl, yth, ytl, hh, hl, dog, bn, bp,
           load_sem, row_send, row_recv, col_send, col_recv, send_sem, recv_sem):
    die, ty, tx = lax.axis_index("die"), lax.axis_index("ty"), lax.axis_index("tx")
    dies, tys, txs = lax.axis_size("die"), lax.axis_size("ty"), lax.axis_size("tx")
    up, down = lax.rem(die + 1, dies), lax.rem(die + dies - 1, dies)
    has_above, has_below, has_left, has_right = ty > 0, ty < tys - 1, tx > 0, tx < txs - 1

    bar = pltpu.get_barrier_semaphore()
    for target in (up, down):
        pl.semaphore_signal(bar, inc=1, device_id={"die": target}, device_id_type=MESH)
    for there, axis, target in ((has_above, "ty", ty - 1), (has_below, "ty", ty + 1), (has_left, "tx", tx - 1), (has_right, "tx", tx + 1)):
        @pl.when(there)
        def _(axis=axis, target=target):
            pl.semaphore_signal(bar, inc=1, device_id={axis: target}, device_id_type=MESH)

    loads = []
    for i, (first, count) in enumerate(((48, 160), (0, 48), (208, 48))):
        copy = pltpu.make_async_copy(x_ref.at[pl.ds(first, count)], pf.at[pl.ds(PAD + first, count), pl.ds(LANE, TW)], load_sem.at[i])
        copy.start()
        loads.append(copy)

    pick = pick_ref[0, 0, 0]
    row_off, col_off = off_ref[0, 0, 0, 0], off_ref[0, 0, 0, 1]
    frac_y = lax.rem(pick, 4).astype(F32) * 0.25 + 0.125
    frac_x = lax.div(pick, 4).astype(F32) * 0.5 + 0.25

    out = lax.broadcasted_iota(jnp.int32, (3 * LANE, LANE), 1)
    step = lax.broadcasted_iota(jnp.int32, (3 * LANE, LANE), 0) - LANE - out - col_off
    for s, sigma in enumerate((1.0, 2.0)):
        wh[:, s * LANE:(s + 1) * LANE], wl[:, s * LANE:(s + 1) * LANE] = split(tap_weights(step, sigma, frac_x))
    for (yh, yl), (_, rows) in (((ych, ycl), CENTER), ((yth, ytl), TOP)):
        span = rows + 2 * PAD
        for s, m in enumerate(row_matrix(rows, row_off, frac_y)):
            yh[:, s * span:(s + 1) * span], yl[:, s * span:(s + 1) * span] = split(m)

    @pl.when(ty == 0)
    def _():
        pf[0:PAD, LANE:LANE + TW] = jnp.zeros((PAD, TW), F32)

    @pl.when(ty == tys - 1)
    def _():
        pf[PAD + TH:, LANE:LANE + TW] = jnp.zeros((PAD, TW), F32)

    @pl.when(tx == 0)
    def _():
        pf[:, 0:LANE] = jnp.zeros((TH + 2 * PAD, LANE), F32)

    @pl.when(tx == txs - 1)
    def _():
        pf[:, LANE + TW:] = jnp.zeros((TH + 2 * PAD, LANE), F32)

    def convert(r0, r1, c0, c1):
        ph[r0:r1, c0:c1], plo[r0:r1, c0:c1] = split(pf[r0:r1, c0:c1])

    def compute(strip, pair):
        first, rows = strip
        span = rows + 2 * PAD
        for n, j in enumerate(pair):
            lanes = slice(j * LANE, (j + 3) * LANE)
            h = product(ph[first:first + span, lanes], plo[first:first + span, lanes], wh[...], wl[...])
            high, low = split(h)
            for s in range(2):
                where = (slice(s * span, (s + 1) * span), slice(n * LANE, (n + 1) * LANE))
                hh[where], hl[where] = high[:, s * LANE:(s + 1) * LANE], low[:, s * LANE:(s + 1) * LANE]
        yh, yl = (ych, ycl) if rows == CENTER[1] else (yth, ytl)
        d = product(yh[...], yl[...], hh[0:2 * span, :], hl[0:2 * span, :])
        for n, j in enumerate(pair):
            dog[first:first + rows, j * LANE:(j + 1) * LANE] = d[:, n * LANE:(n + 1) * LANE]

    pieces = []

    def send(strip, pair):
        first, rows = strip
        spots = [(pair[0], 2)] if pair[1] == pair[0] + 1 else [(j, 1) for j in pair]
        for j, blocks in spots:
            i = len(pieces)
            where = (pl.ds(first, rows), pl.ds(j * LANE, blocks * LANE))
            copies = []
            for k, (target, landing) in enumerate(((down, bn), (up, bp))):
                copy = pltpu.make_async_remote_copy(src_ref=dog.at[where], dst_ref=landing.at[where], send_sem=send_sem.at[k, i],
                                                    recv_sem=recv_sem.at[k, i], device_id={"die": target}, device_id_type=MESH)
                copy.start()
                copies.append(copy)
            pieces.append((where, copies))

    loads[0].wait()
    convert(64, 224, LANE, LANE + TW)
    compute(CENTER, INNER[0])
    pl.semaphore_wait(bar, 2 + has_above.astype(jnp.int32) + has_below.astype(jnp.int32) + has_left.astype(jnp.int32) + has_right.astype(jnp.int32))
    send(CENTER, INNER[0])

    loads[1].wait()
    loads[2].wait()
    core = pl.ds(LANE, TW)
    to_above = pltpu.make_async_remote_copy(src_ref=pf.at[pl.ds(PAD, PAD), core], dst_ref=pf.at[pl.ds(PAD + TH, PAD), core],
                                            send_sem=row_send.at[0], recv_sem=row_recv.at[0], device_id={"ty": ty - 1}, device_id_type=MESH)
    to_below = pltpu.make_async_remote_copy(src_ref=pf.at[pl.ds(TH, PAD), core], dst_ref=pf.at[pl.ds(0, PAD), core],
                                            send_sem=row_send.at[1], recv_sem=row_recv.at[1], device_id={"ty": ty + 1}, device_id_type=MESH)
    pl.when(has_above)(lambda: to_above.start())
    pl.when(has_below)(lambda: to_below.start())

    for pair in INNER[1:]:
        compute(CENTER, pair)
        send(CENTER, pair)

    pl.when(has_below)(lambda: to_above.wait_recv())
    pl.when(has_above)(lambda: to_below.wait_recv())
    to_left = pltpu.make_async_remote_copy(src_ref=pf.at[:, pl.ds(LANE, LANE)], dst_ref=pf.at[:, pl.ds(LANE + TW, LANE)],
                                           send_sem=col_send.at[0], recv_sem=col_recv.at[0], device_id={"tx": tx - 1}, device_id_type=MESH)
    to_right = pltpu.make_async_remote_copy(src_ref=pf.at[:, pl.ds(TW, LANE)], dst_ref=pf.at[:, pl.ds(0, LANE)],
                                            send_sem=col_send.at[1], recv_sem=col_recv.at[1], device_id={"tx": tx + 1}, device_id_type=MESH)
    pl.when(has_left)(lambda: to_left.start())
    pl.when(has_right)(lambda: to_right.start())

    convert(0, 64, LANE, LANE + TW)
    convert(224, 288, LANE, LANE + TW)
    for strip in (TOP, BOTTOM):
        for pair in INNER:
            compute(strip, pair)
            send(strip, pair)

    pl.when(has_right)(lambda: to_left.wait_recv())
    pl.when(has_left)(lambda: to_right.wait_recv())
    convert(0, 288, 0, LANE)
    convert(0, 288, LANE + TW, 2 * LANE + TW)
    for strip in (CENTER, TOP, BOTTOM):
        compute(strip, OUTER)
        send(strip, OUTER)

    not_last, not_first = die < dies - 1, die > 0
    for where, (from_next, from_prev) in pieces:
        from_next.wait_recv()
        next_ref[where] = jnp.where(not_last, bn[where] - dog[where], 0.0)
        from_prev.wait_recv()
        prev_ref[where] = jnp.where(not_first, dog[where] - bp[where], 0.0)
    for _, copies in pieces:
        for copy in copies:
            copy.wait_send()
    pl.when(has_above)(lambda: to_above.wait_send())
    pl.when(has_below)(lambda: to_below.wait_send())
    pl.when(has_left)(lambda: to_left.wait_send())
    pl.when(has_right)(lambda: to_right.wait_send())


N_PIECES = 3 * len(INNER) + 6


def body(raster, shift_pick, offsets):
    tile = jax.ShapeDtypeStruct((TH, TW), F32)
    wide, high = TW + 2 * LANE, TH + 2 * PAD
    dma = pltpu.SemaphoreType.DMA
    center, edge = CENTER[1] + 2 * PAD, TOP[1] + 2 * PAD
    next_map, prev_map = pl.pallas_call(
        kernel,
        out_shape=[tile, tile],
        in_specs=[pl.BlockSpec(memory_space=pltpu.SMEM), pl.BlockSpec(memory_space=pltpu.SMEM), pl.BlockSpec(memory_space=pltpu.HBM)],
        out_specs=[pl.BlockSpec(memory_space=pltpu.VMEM)] * 2,
        scratch_shapes=[
            pltpu.VMEM((high, wide), F32), pltpu.VMEM((high, wide), BF16), pltpu.VMEM((high, wide), BF16),
            pltpu.VMEM((3 * LANE, 2 * LANE), BF16), pltpu.VMEM((3 * LANE, 2 * LANE), BF16),
            pltpu.VMEM((CENTER[1], 2 * center), BF16), pltpu.VMEM((CENTER[1], 2 * center), BF16),
            pltpu.VMEM((TOP[1], 2 * edge), BF16), pltpu.VMEM((TOP[1], 2 * edge), BF16),
            pltpu.VMEM((2 * center, 2 * LANE), BF16), pltpu.VMEM((2 * center, 2 * LANE), BF16),
            pltpu.VMEM((TH, TW), F32), pltpu.VMEM((TH, TW), F32), pltpu.VMEM((TH, TW), F32),
            dma((3,)), dma((2,)), dma((2,)), dma((2,)), dma((2,)), dma((2, N_PIECES)), dma((2, N_PIECES)),
        ],
        compiler_params=pltpu.CompilerParams(collective_id=0, has_side_effects=True, vmem_limit_bytes=32 * 1024 * 1024),
    )(shift_pick, offsets, raster[0])
    return next_map[None], prev_map[None]


def solution(mesh):
    in_specs = (P("die", "ty", "tx"), P("die", "ty", "tx"), P("die", "ty", "tx", None))
    out_specs = (P("die", "ty", "tx"), P("die", "ty", "tx"))
    return jax.shard_map(body, mesh=mesh, in_specs=in_specs, out_specs=out_specs, check_vma=False)
```

time: 126 us -> 42.8 us (0.34)
  the two profiles are of different devices: /device:TPU:7 before, /device:TPU:1 now
where the time goes in v1:
time: 42.8 us; the launch traced here: 42.6 us
  Pallas kernels  37.5 us (88%)
  local copies, waits for them, and re-layouts  3.81 us (9%)
  between operations  1.29 us (3%)
    pallas_call x1, Pallas kernels, body(): pl.pallas_call(kernel, out_shape=[tile, tile], in_specs=[pl.BlockSpec(mem...  37.5 us
    unnamed x6, local copies, waits for them, and re-layouts  3.81 us

profile of v1, /device:TPU:1, one launch (start us, length us, event | category | flops | bytes accessed | tf_op | source)
XLA Modules:
  0.0 42.6 jit_solution(10588615463186400422)
XLA Ops:
  1.3 0.0 copy-start.1
  1.3 0.6 %copy-done.1 = s32[1,1,1,2]{3,2,1,0:T(1,128)S(1)} copy-done((s32[1,1,1,2]{3,2,1,0:T(1,128)S(1)}, s32[1,1,1,2]{3,2,1,0:T(1,128)}, u32[]{:S(2)}) %copy-start.1) | copy-done | bytes 32
  1.9 0.0 copy-start
  1.9 1.2 %copy-done = f32[1,256,1024]{2,1,0:T(8,128)S(1)} copy-done((f32[1,256,1024]{2,1,0:T(8,128)S(1)}, f32[1,256,1024]{2,1,0:T(8,128)}, u32[]{:S(2)}) %copy-start) | copy-done | bytes 1048600
  3.2 37.5 %shard_map.50 = (f32[256,1024]{1,0:T(8,128)S(1)}, f32[256,1024]{1,0:T(8,128)S(1)}) custom-call(s32[1,1,1]{2,1,0:T(1,128)S(6)} %copy.7.pick_ref, s32[1,1,1,2]{3,2,1,0:T(1,128)S(1)} %copy-done.1, f32[256,1024]{1,0:T(8,128)S(1)} %bitcast.3), custom_call_target="tpu_custom_call" | custom-call | tf_op jit(solution)/shard_map/pallas_call | solution.py:202
  40.7 1.0 %copy.8 = f32[1,256,1024]{2,1,0:T(8,128)} copy(f32[1,256,1024]{2,1,0:T(8,128)S(1)} %bitcast.5) | data formatting | bytes 2097152
  41.6 1.0 %copy.9 = f32[1,256,1024]{2,1,0:T(8,128)} copy(f32[1,256,1024]{2,1,0:T(8,128)S(1)} %bitcast.4) | data formatting | bytes 2097152
Async XLA Ops:
  1.3 0.7 %copy-start.1 = (s32[1,1,1,2]{3,2,1,0:T(1,128)S(1)}, s32[1,1,1,2]{3,2,1,0:T(1,128)}, u32[]{:S(2)}) copy-start(s32[1,1,1,2]{3,2,1,0:T(1,128)} %off_ref.1) | copy-start | bytes 28
  1.9 1.2 %copy-start = (f32[1,256,1024]{2,1,0:T(8,128)S(1)}, f32[1,256,1024]{2,1,0:T(8,128)}, u32[]{:S(2)}) copy-start(f32[1,256,1024]{2,1,0:T(8,128)} %param.3) | copy-start | bytes 3145732

commit v2 on v1

--- a/solution.py
+++ b/solution.py
@@ -47,27 +47,30 @@
     return tap_weights(step, 1.0, frac_y), -tap_weights(step, 2.0, frac_y)
 
 
-def kernel(pick_ref, off_ref, x_ref, next_ref, prev_ref, pf, ph, plo, wh, wl, ych, ycl, yth, ytl, hh, hl, dog, bn, bp,
-           load_sem, row_send, row_recv, col_send, col_recv, send_sem, recv_sem):
+def kernel(pick_ref, off_hbm, x_ref, next_ref, prev_ref, off_ref, pf, ph, plo, wh, wl, ych, ycl, yth, ytl, hh, hl, dog, bn, bp,
+           load_sem, row_send, row_recv, col_send, col_recv, send_sem, recv_sem, ready):
     die, ty, tx = lax.axis_index("die"), lax.axis_index("ty"), lax.axis_index("tx")
     dies, tys, txs = lax.axis_size("die"), lax.axis_size("ty"), lax.axis_size("tx")
-    up, down = lax.rem(die + 1, dies), lax.rem(die + dies - 1, dies)
+    has_next, has_prev = die < dies - 1, die > 0
     has_above, has_below, has_left, has_right = ty > 0, ty < tys - 1, tx > 0, tx < txs - 1
 
     bar = pltpu.get_barrier_semaphore()
-    for target in (up, down):
-        pl.semaphore_signal(bar, inc=1, device_id={"die": target}, device_id_type=MESH)
-    for there, axis, target in ((has_above, "ty", ty - 1), (has_below, "ty", ty + 1), (has_left, "tx", tx - 1), (has_right, "tx", tx + 1)):
+    odd = lax.rem(tx, 2) == 1
+    beside = ((has_left, tx - 1), (has_right, tx + 1))
+    for there, axis, target in ((has_next, "die", die + 1), (has_prev, "die", die - 1), (has_above, "ty", ty - 1), (has_below, "ty", ty + 1)):
         @pl.when(there)
         def _(axis=axis, target=target):
             pl.semaphore_signal(bar, inc=1, device_id={axis: target}, device_id_type=MESH)
 
+    small = pltpu.make_async_copy(off_hbm, off_ref, load_sem.at[3])
+    small.start()
     loads = []
     for i, (first, count) in enumerate(((48, 160), (0, 48), (208, 48))):
         copy = pltpu.make_async_copy(x_ref.at[pl.ds(first, count)], pf.at[pl.ds(PAD + first, count), pl.ds(LANE, TW)], load_sem.at[i])
         copy.start()
         loads.append(copy)
 
+    small.wait()
     pick = pick_ref[0, 0, 0]
     row_off, col_off = off_ref[0, 0, 0, 0], off_ref[0, 0, 0, 1]
     frac_y = lax.rem(pick, 4).astype(F32) * 0.25 + 0.125
@@ -125,18 +128,28 @@
             i = len(pieces)
             where = (pl.ds(first, rows), pl.ds(j * LANE, blocks * LANE))
             copies = []
-            for k, (target, landing) in enumerate(((down, bn), (up, bp))):
+            for k, (there, target, landing) in enumerate(((has_prev, die - 1, bn), (has_next, die + 1, bp))):
                 copy = pltpu.make_async_remote_copy(src_ref=dog.at[where], dst_ref=landing.at[where], send_sem=send_sem.at[k, i],
                                                     recv_sem=recv_sem.at[k, i], device_id={"die": target}, device_id_type=MESH)
-                copy.start()
+                pl.when(there)(copy.start)
                 copies.append(copy)
             pieces.append((where, copies))
 
     loads[0].wait()
     convert(64, 224, LANE, LANE + TW)
     compute(CENTER, INNER[0])
-    pl.semaphore_wait(bar, 2 + has_above.astype(jnp.int32) + has_below.astype(jnp.int32) + has_left.astype(jnp.int32) + has_right.astype(jnp.int32))
+    count = lambda *flags: sum(flag.astype(jnp.int32) for flag in flags)
+    tx_count = count(has_left, has_right)
+    pl.semaphore_wait(bar, count(has_next, has_prev, has_above, has_below) + jnp.where(odd, 0, tx_count))
     send(CENTER, INNER[0])
+    for there, target in beside:
+        @pl.when(there & odd)
+        def _(target=target):
+            pl.semaphore_signal(bar, inc=1, device_id={"tx": target}, device_id_type=MESH)
+
+        @pl.when(there & jnp.logical_not(odd))
+        def _(target=target):
+            pl.semaphore_signal(ready, inc=1, device_id={"tx": target}, device_id_type=MESH)
 
     loads[1].wait()
     loads[2].wait()
@@ -158,6 +171,7 @@
                                            send_sem=col_send.at[0], recv_sem=col_recv.at[0], device_id={"tx": tx - 1}, device_id_type=MESH)
     to_right = pltpu.make_async_remote_copy(src_ref=pf.at[:, pl.ds(TW, LANE)], dst_ref=pf.at[:, pl.ds(0, LANE)],
                                             send_sem=col_send.at[1], recv_sem=col_recv.at[1], device_id={"tx": tx + 1}, device_id_type=MESH)
+    pl.when(odd)(lambda: pl.semaphore_wait(ready, tx_count))
     pl.when(has_left)(lambda: to_left.start())
     pl.when(has_right)(lambda: to_right.start())
 
@@ -176,19 +190,42 @@
         compute(strip, OUTER)
         send(strip, OUTER)
 
-    not_last, not_first = die < dies - 1, die > 0
-    for where, (from_next, from_prev) in pieces:
-        from_next.wait_recv()
-        next_ref[where] = jnp.where(not_last, bn[where] - dog[where], 0.0)
-        from_prev.wait_recv()
-        prev_ref[where] = jnp.where(not_first, dog[where] - bp[where], 0.0)
-    for _, copies in pieces:
-        for copy in copies:
-            copy.wait_send()
+    for there, ref in ((has_next, next_ref), (has_prev, prev_ref)):
+        @pl.when(jnp.logical_not(there))
+        def _(ref=ref):
+            ref[...] = jnp.zeros((TH, TW), F32)
+
+    for where, (to_prev, to_next) in pieces:
+        @pl.when(has_next)
+        def _(where=where, arrival=to_prev):
+            arrival.wait_recv()
+            next_ref[where] = bn[where] - dog[where]
+
+        @pl.when(has_prev)
+        def _(where=where, arrival=to_next):
+            arrival.wait_recv()
+            prev_ref[where] = dog[where] - bp[where]
+
+    for _, (to_prev, to_next) in pieces:
+        pl.when(has_prev)(to_prev.wait_send)
+        pl.when(has_next)(to_next.wait_send)
     pl.when(has_above)(lambda: to_above.wait_send())
     pl.when(has_below)(lambda: to_below.wait_send())
     pl.when(has_left)(lambda: to_left.wait_send())
     pl.when(has_right)(lambda: to_right.wait_send())
+
+
+def flush(next_in, prev_in, next_out, prev_out, sem):
+    parts = 4
+    copies = []
+    for k, (source, target) in enumerate(((next_in, next_out), (prev_in, prev_out))):
+        for i in range(parts):
+            rows = pl.ds(i * (TH // parts), TH // parts)
+            copies.append(pltpu.make_async_copy(source.at[rows], target.at[rows], sem.at[k, i]))
+    for copy in copies:
+        copy.start()
+    for copy in copies:
+        copy.wait()
 
 
 N_PIECES = 3 * len(INNER) + 6
@@ -202,20 +239,29 @@
     next_map, prev_map = pl.pallas_call(
         kernel,
         out_shape=[tile, tile],
-        in_specs=[pl.BlockSpec(memory_space=pltpu.SMEM), pl.BlockSpec(memory_space=pltpu.SMEM), pl.BlockSpec(memory_space=pltpu.HBM)],
+        in_specs=[pl.BlockSpec(memory_space=pltpu.SMEM)] + [pl.BlockSpec(memory_space=pltpu.HBM)] * 2,
         out_specs=[pl.BlockSpec(memory_space=pltpu.VMEM)] * 2,
         scratch_shapes=[
+            pltpu.SMEM((1, 1, 1, 2), jnp.int32),
             pltpu.VMEM((high, wide), F32), pltpu.VMEM((high, wide), BF16), pltpu.VMEM((high, wide), BF16),
             pltpu.VMEM((3 * LANE, 2 * LANE), BF16), pltpu.VMEM((3 * LANE, 2 * LANE), BF16),
             pltpu.VMEM((CENTER[1], 2 * center), BF16), pltpu.VMEM((CENTER[1], 2 * center), BF16),
             pltpu.VMEM((TOP[1], 2 * edge), BF16), pltpu.VMEM((TOP[1], 2 * edge), BF16),
             pltpu.VMEM((2 * center, 2 * LANE), BF16), pltpu.VMEM((2 * center, 2 * LANE), BF16),
             pltpu.VMEM((TH, TW), F32), pltpu.VMEM((TH, TW), F32), pltpu.VMEM((TH, TW), F32),
-            dma((3,)), dma((2,)), dma((2,)), dma((2,)), dma((2,)), dma((2, N_PIECES)), dma((2, N_PIECES)),
+            dma((4,)), dma((2,)), dma((2,)), dma((2,)), dma((2,)), dma((2, N_PIECES)), dma((2, N_PIECES)), pltpu.SemaphoreType.REGULAR,
         ],
         compiler_params=pltpu.CompilerParams(collective_id=0, has_side_effects=True, vmem_limit_bytes=32 * 1024 * 1024),
-    )(shift_pick, offsets, raster[0])
-    return next_map[None], prev_map[None]
+    )(shift_pick, *(pltpu.with_memory_space_constraint(x, pltpu.HBM) for x in (offsets, raster[0])))
+    maps = pl.pallas_call(
+        flush,
+        out_shape=[tile, tile],
+        in_specs=[pl.BlockSpec(memory_space=pltpu.VMEM)] * 2,
+        out_specs=[pl.BlockSpec(memory_space=pltpu.HBM)] * 2,
+        scratch_shapes=[dma((2, 4))],
+        compiler_params=pltpu.CompilerParams(vmem_limit_bytes=4 * 1024 * 1024),
+    )(*(pltpu.with_memory_space_constraint(x, pltpu.VMEM) for x in (next_map, prev_map)))
+    return maps[0][None], maps[1][None]
 
 
 def solution(mesh):

time: 42.8 us -> 33.5 us (0.78)
  the two profiles are of different devices: /device:TPU:1 before, /device:TPU:7 now
where the time goes in v2:
time: 33.5 us; the launch traced here: 33.1 us
  Pallas kernels  31.8 us (95%)
  between operations  1.28 us (4%)
    pallas_call x1, Pallas kernels, body(): pl.pallas_call(kernel, out_shape=[tile, tile], in_specs=[pl.BlockSpec(mem...  30.5 us
    pallas_call x1, Pallas kernels, body(): pl.pallas_call(flush, out_shape=[tile, tile], in_specs=[pl.BlockSpec(memo...  1.38 us

profile of v2, /device:TPU:7, one launch (start us, length us, event | category | flops | bytes accessed | tf_op | source)
XLA Modules:
  0.0 33.1 jit_solution(8943120520252199041)
XLA Ops:
  1.3 30.5 %shard_map.50 = (f32[256,1024]{1,0:T(8,128)S(1)}, f32[256,1024]{1,0:T(8,128)S(1)}) custom-call(s32[1,1,1]{2,1,0:T(1,128)S(6)} %copy.5.pick_ref, s32[1,1,1,2]{3,2,1,0:T(1,128)} %off_hbm.1, f32[256,1024]{1,0:T(8,128)} %bitcast.3), custom_call_target="tpu_custom_call" | custom-call | tf_op jit(solution)/shard_map/pallas_call | solution.py:239
  31.8 1.4 %shard_map.51 = (f32[256,1024]{1,0:T(8,128)}, f32[256,1024]{1,0:T(8,128)}) custom-call(f32[256,1024]{1,0:T(8,128)S(1)} %get-tuple-element.6.next_in, f32[256,1024]{1,0:T(8,128)S(1)} %get-tuple-element.7.prev_in), custom_call_target="tpu_custom_call" | custom-call | tf_op jit(solution)/shard_map/pallas_call | solution.py:256

commit v3 on v2

v3 whole, which is shorter than its diff:
```python
import functools
import math

import jax
import jax.numpy as jnp
from jax import lax
from jax.experimental import pallas as pl
from jax.experimental.pallas import tpu as pltpu
from jax.sharding import PartitionSpec as P

MESH = pl.DeviceIdType.MESH
F32, BF16 = jnp.float32, jnp.bfloat16
TH, TW = 256, 1024
RG = 6
PAD = 16
LANE = 128
ROWS = 64
SPAN = ROWS + 2 * PAD
UPPER, LOWER, TOP, BOTTOM = 64, 128, 0, 192
INNER = ((1, 2), (3, 4), (5, 6))
OUTER = (0, 7)
GROUPS = (((64, 64, 1, 1), (64, 64, 2, 1), (128, 64, 1, 2), (64, 128, 3, 2), (64, 128, 5, 2)),
          ((0, 64, 1, 6), (192, 64, 1, 6)),
          ((0, 256, 0, 1), (0, 256, 7, 1)))
ARRIVALS = ((128, 768), (128, 768), (256, 256))


def start_rank(die, ty, tx):
    late_first = jnp.where((die == 0) & (ty == 0) & (tx == 0), 50, 0)
    return 13 * ty + 50 * lax.div(tx, 2) - 4 * lax.rem(tx, 2) + late_first


def tap_weights(step, sigma, frac):
    norm = sum(math.exp(-k * k / (2.0 * sigma * sigma)) for k in range(-RG, RG + 1))

    def gauss(k):
        spot = k.astype(F32)
        value = jnp.exp(spot * spot * (-1.0 / (2.0 * sigma * sigma))) * (1.0 / norm)
        return jnp.where(jnp.abs(k) <= RG, value, 0.0)

    return (1.0 - frac) * gauss(step) + frac * gauss(step - 1)


def split(x):
    high = x.astype(BF16)
    return high, (x - high.astype(F32)).astype(BF16)


def product(ah, al, bh, bl):
    dot = functools.partial(jnp.dot, preferred_element_type=F32)
    return dot(ah, bh) + dot(ah, bl) + dot(al, bh)


def kernel(pick_ref, off_hbm, x_ref, next_ref, prev_ref, off_ref, pf, ph, plo, wh, wl, yh, yl, hh, hl, dog, bn, bp,
           load_sem, row_send, row_recv, col_send, col_recv, send_sem, recv_sem, ready):
    die, ty, tx = lax.axis_index("die"), lax.axis_index("ty"), lax.axis_index("tx")
    dies, tys, txs = lax.axis_size("die"), lax.axis_size("ty"), lax.axis_size("tx")
    has_next, has_prev = die < dies - 1, die > 0
    bar = pltpu.get_barrier_semaphore()
    for flag, target in ((has_next, die + 1), (has_prev, die - 1)):
        @pl.when(flag)
        def _(target=target):
            pl.semaphore_signal(bar, inc=1, device_id={"die": target}, device_id_type=MESH)

    has_above, has_below, has_left, has_right = ty > 0, ty < tys - 1, tx > 0, tx < txs - 1
    count = lambda flags: sum(flag.astype(jnp.int32) for flag in flags)

    here = start_rank(die, ty, tx)
    sides = (({"ty": ty + 1}, has_below, (die, ty + 1, tx), 1), ({"ty": ty - 1}, has_above, (die, ty - 1, tx), 0),
             ({"tx": tx + 1}, has_right, (die, ty, tx + 1), 3), ({"tx": tx - 1}, has_left, (die, ty, tx - 1), 2))
    follows = [there & (start_rank(*spot) > here) for _, there, spot, _ in sides]
    leads = [there & (start_rank(*spot) < here) for _, there, spot, _ in sides]
    BELOW, ABOVE, RIGHT, LEFT = range(4)

    def await_follower(side):
        pl.when(follows[side])(lambda: pl.semaphore_wait(ready.at[side], 1))

    for (target, _, _, _), flag in zip(sides, follows):
        @pl.when(flag)
        def _(target=target):
            pl.semaphore_signal(bar, inc=1, device_id=target, device_id_type=MESH)

    small = pltpu.make_async_copy(off_hbm, off_ref, load_sem.at[0])
    small.start()
    loads = []
    for i, (first, rows, left, columns) in enumerate(((48, 96, 0, 512), (144, 64, 0, 512), (48, 160, 512, 512), (0, 48, 0, TW), (208, 48, 0, TW))):
        copy = pltpu.make_async_copy(x_ref.at[pl.ds(first, rows), pl.ds(left, columns)],
                                     pf.at[pl.ds(PAD + first, rows), pl.ds(LANE + left, columns)], load_sem.at[min(i + 1, 4)])
        copy.start()
        loads.append(copy)
    edges = pltpu.make_async_copy(x_ref.at[pl.ds(0, 96)], pf.at[pl.ds(PAD, 96), pl.ds(LANE, TW)], load_sem.at[4])

    band = slice(LANE - PAD, 2 * LANE + PAD)
    for w in (wh, wl):
        w[0:LANE - PAD, :] = jnp.zeros((LANE - PAD, 2 * LANE), BF16)
        w[2 * LANE + PAD:, :] = jnp.zeros((LANE - PAD, 2 * LANE), BF16)
    pick = pick_ref[0, 0, 0]
    frac_y = lax.rem(pick, 4).astype(F32) * 0.25 + 0.125
    frac_x = lax.div(pick, 4).astype(F32) * 0.5 + 0.25
    small.wait()
    row_off, col_off = off_ref[0, 0, 0, 0], off_ref[0, 0, 0, 1]
    iota = lambda shape, dim: lax.broadcasted_iota(jnp.int32, shape, dim)
    step = iota((LANE + 2 * PAD, LANE), 0) - PAD - iota((LANE + 2 * PAD, LANE), 1) - col_off
    for s, sigma in enumerate((1.0, 2.0)):
        lanes = slice(s * LANE, (s + 1) * LANE)
        wh[band, lanes], wl[band, lanes] = split(tap_weights(step, sigma, frac_x))
    column = iota((ROWS, 2 * SPAN), 1)
    step = jnp.where(column < SPAN, column, column - SPAN) - PAD - iota((ROWS, 2 * SPAN), 0) - row_off
    yh[...], yl[...] = split(jnp.where(column < SPAN, tap_weights(step, 1.0, frac_y), -tap_weights(step, 2.0, frac_y)))

    def convert(r0, r1, c0, c1):
        ph[r0:r1, c0:c1], plo[r0:r1, c0:c1] = split(pf[r0:r1, c0:c1])

    def compute(first, pair):
        for n, j in enumerate(pair):
            lanes = slice(j * LANE, (j + 3) * LANE)
            h = product(ph[first:first + SPAN, lanes], plo[first:first + SPAN, lanes], wh[...], wl[...])
            high, low = split(h)
            for s in range(2):
                where = (slice(s * SPAN, (s + 1) * SPAN), slice(n * LANE, (n + 1) * LANE))
                hh[where], hl[where] = high[:, s * LANE:(s + 1) * LANE], low[:, s * LANE:(s + 1) * LANE]
        wide = slice(0, len(pair) * LANE)
        d = product(yh[...], yl[...], hh[:, wide], hl[:, wide])
        for n, j in enumerate(pair):
            dog[first:first + ROWS, j * LANE:(j + 1) * LANE] = d[:, n * LANE:(n + 1) * LANE]

    def transfer(k, group, where):
        target, landing = ((die - 1, bn), (die + 1, bp))[k]
        return pltpu.make_async_remote_copy(src_ref=dog.at[where], dst_ref=landing.at[where], send_sem=send_sem.at[k], recv_sem=recv_sem.at[k, group],
                                            device_id={"die": target}, device_id_type=MESH)

    spots = [[(pl.ds(first, rows), pl.ds(left * LANE, blocks * LANE)) for first, rows, left, blocks in group] for group in GROUPS]
    pieces = [[transfer(k, g, where) for k in range(2)] for g, group in enumerate(spots) for where in group]

    def send(i):
        to_prev, to_next = pieces[i]
        pl.when(has_prev)(to_prev.start)
        pl.when(has_next)(to_next.start)

    core = pl.ds(LANE, TW)
    to_above, to_below = (
        pltpu.make_async_remote_copy(src_ref=pf.at[pl.ds(source, PAD), core], dst_ref=pf.at[pl.ds(target, PAD), core], send_sem=row_send.at[i],
                                     recv_sem=row_recv.at[i], device_id={"ty": to}, device_id_type=MESH)
        for i, (source, target, to) in enumerate(((PAD, PAD + TH, ty - 1), (TH, 0, ty + 1))))
    parts = (pl.ds(PAD, TH), pl.ds(0, PAD), pl.ds(PAD + TH, PAD), pl.ds(0, TH + 2 * PAD))
    to_left, to_right = (
        [pltpu.make_async_remote_copy(src_ref=pf.at[rows, pl.ds(source, LANE)], dst_ref=pf.at[rows, pl.ds(target, LANE)], send_sem=col_send.at[i],
                                      recv_sem=col_recv.at[i], device_id={"tx": to}, device_id_type=MESH) for rows in parts]
        for i, (source, target, to) in enumerate(((LANE, LANE + TW, tx - 1), (TW, 0, tx + 1))))

    loads[0].wait()
    convert(64, 160, LANE, LANE + 512)
    compute(UPPER, INNER[0][:1])
    pl.semaphore_wait(bar, count([has_next, has_prev] + leads))
    for (target, _, _, slot), flag in zip(sides, leads):
        @pl.when(flag)
        def _(target=target, slot=slot):
            pl.semaphore_signal(ready.at[slot], inc=1, device_id=target, device_id_type=MESH)

    send(0)
    compute(UPPER, INNER[0][1:])
    send(1)
    loads[1].wait()
    convert(160, 224, LANE, LANE + 512)
    compute(LOWER, INNER[0])
    send(2)
    loads[2].wait()
    edges.wait()
    pl.when(leads[ABOVE])(to_above.start)
    pl.when(leads[BELOW])(to_below.start)
    pl.when(leads[LEFT])(to_left[0].start)
    pl.when(leads[RIGHT])(to_right[0].start)
    convert(64, 224, LANE + 512, LANE + TW)
    for i, pair in enumerate(INNER[1:]):
        compute(UPPER, pair)
        compute(LOWER, pair)
        send(3 + i)
    for side, copy in ((BELOW, to_below), (ABOVE, to_above)):
        await_follower(side)
        pl.when(follows[side])(copy.start)

    @pl.when(ty == 0)
    def _():
        pf[0:PAD, LANE:LANE + TW] = jnp.zeros((PAD, TW), F32)

    @pl.when(ty == tys - 1)
    def _():
        pf[PAD + TH:, LANE:LANE + TW] = jnp.zeros((PAD, TW), F32)

    pl.when(has_below)(to_above.wait_recv)
    pl.when(has_above)(to_below.wait_recv)
    for i in (1, 2):
        pl.when(leads[LEFT])(to_left[i].start)
        pl.when(leads[RIGHT])(to_right[i].start)
    convert(0, 64, LANE, LANE + TW)
    convert(224, 288, LANE, LANE + TW)
    for i, first in enumerate((TOP, BOTTOM)):
        for pair in INNER:
            compute(first, pair)
        send(5 + i)

    for side, copies in ((RIGHT, to_right), (LEFT, to_left)):
        await_follower(side)
        for copy in copies[:3]:
            pl.when(follows[side])(copy.start)

    @pl.when(tx == 0)
    def _():
        pf[:, 0:LANE] = jnp.zeros((TH + 2 * PAD, LANE), F32)

    @pl.when(tx == txs - 1)
    def _():
        pf[:, LANE + TW:] = jnp.zeros((TH + 2 * PAD, LANE), F32)

    pl.when(has_right)(to_left[3].wait_recv)
    pl.when(has_left)(to_right[3].wait_recv)
    convert(0, 288, 0, LANE)
    convert(0, 288, LANE + TW, 2 * LANE + TW)
    for first in (TOP, UPPER, LOWER, BOTTOM):
        compute(first, OUTER)
    send(7)
    send(8)

    for there, ref in ((has_next, next_ref), (has_prev, prev_ref)):
        @pl.when(jnp.logical_not(there))
        def _(ref=ref):
            ref[...] = jnp.zeros((TH, TW), F32)

    for g, (group, (rows, columns)) in enumerate(zip(spots, ARRIVALS)):
        block = (pl.ds(0, rows), pl.ds(0, columns))

        @pl.when(has_next)
        def _(g=g, group=group, block=block):
            transfer(0, g, block).wait_recv()
            for where in group:
                next_ref[where] = bn[where] - dog[where]

        @pl.when(has_prev)
        def _(g=g, group=group, block=block):
            transfer(1, g, block).wait_recv()
            for where in group:
                prev_ref[where] = dog[where] - bp[where]

    tile = (pl.ds(0, TH), pl.ds(0, TW))
    pl.when(has_prev)(transfer(0, 0, tile).wait_send)
    pl.when(has_next)(transfer(1, 0, tile).wait_send)
    pl.when(has_above)(to_above.wait_send)
    pl.when(has_below)(to_below.wait_send)
    pl.when(has_left)(to_left[3].wait_send)
    pl.when(has_right)(to_right[3].wait_send)


def flush(next_in, prev_in, next_out, prev_out, sem):
    copies = [pltpu.make_async_copy(next_in, next_out, sem.at[0]), pltpu.make_async_copy(prev_in, prev_out, sem.at[1])]
    for copy in copies:
        copy.start()
    for copy in copies:
        copy.wait()


def body(raster, shift_pick, offsets):
    tile = jax.ShapeDtypeStruct((TH, TW), F32)
    wide, high = TW + 2 * LANE, TH + 2 * PAD
    dma = pltpu.SemaphoreType.DMA
    next_map, prev_map = pl.pallas_call(
        kernel,
        out_shape=[tile, tile],
        in_specs=[pl.BlockSpec(memory_space=pltpu.SMEM)] + [pl.BlockSpec(memory_space=pltpu.HBM)] * 2,
        out_specs=[pl.BlockSpec(memory_space=pltpu.VMEM)] * 2,
        scratch_shapes=[
            pltpu.SMEM((1, 1, 1, 2), jnp.int32),
            pltpu.VMEM((high, wide), F32), pltpu.VMEM((high, wide), BF16), pltpu.VMEM((high, wide), BF16),
            pltpu.VMEM((3 * LANE, 2 * LANE), BF16), pltpu.VMEM((3 * LANE, 2 * LANE), BF16),
            pltpu.VMEM((ROWS, 2 * SPAN), BF16), pltpu.VMEM((ROWS, 2 * SPAN), BF16),
            pltpu.VMEM((2 * SPAN, 2 * LANE), BF16), pltpu.VMEM((2 * SPAN, 2 * LANE), BF16),
            pltpu.VMEM((TH, TW), F32), pltpu.VMEM((TH, TW), F32), pltpu.VMEM((TH, TW), F32),
            dma((5,)), dma((2,)), dma((2,)), dma((2,)), dma((2,)), dma((2,)), dma((2, 3)), pltpu.SemaphoreType.REGULAR((4,)),
        ],
        compiler_params=pltpu.CompilerParams(collective_id=0, has_side_effects=True, vmem_limit_bytes=32 * 1024 * 1024),
    )(shift_pick, *(pltpu.with_memory_space_constraint(x, pltpu.HBM) for x in (offsets, raster[0])))
    maps = pl.pallas_call(
        flush,
        out_shape=[tile, tile],
        in_specs=[pl.BlockSpec(memory_space=pltpu.VMEM)] * 2,
        out_specs=[pl.BlockSpec(memory_space=pltpu.HBM)] * 2,
        scratch_shapes=[dma((2,))],
        compiler_params=pltpu.CompilerParams(vmem_limit_bytes=4 * 1024 * 1024),
    )(*(pltpu.with_memory_space_constraint(x, pltpu.VMEM) for x in (next_map, prev_map)))
    return maps[0][None], maps[1][None]


def solution(mesh):
    in_specs = (P("die", "ty", "tx"), P("die", "ty", "tx"), P("die", "ty", "tx", None))
    out_specs = (P("die", "ty", "tx"), P("die", "ty", "tx"))
    return jax.shard_map(body, mesh=mesh, in_specs=in_specs, out_specs=out_specs, check_vma=False)
```

time: 33.5 us -> 32.4 us (0.967)
  Pallas kernels: 31.8 us -> 30.9 us
    pallas_call x1, Pallas kernels: 30.5 us -> 29.6 us  [body(): pl.pallas_call(kernel, out_shape=[tile, tile], in_specs=[pl.BlockSpec(mem...]
where the time goes in v3:
time: 32.4 us; the launch traced here: 32.2 us
  Pallas kernels  30.9 us (95%)
  between operations  1.28 us (4%)
    pallas_call x1, Pallas kernels, body(): pl.pallas_call(kernel, out_shape=[tile, tile], in_specs=[pl.BlockSpec(mem...  29.6 us
    pallas_call x1, Pallas kernels, body(): pl.pallas_call(flush, out_shape=[tile, tile], in_specs=[pl.BlockSpec(memo...  1.33 us

profile of v3, /device:TPU:7, one launch (start us, length us, event | category | flops | bytes accessed | tf_op | source)
XLA Modules:
  0.0 32.2 jit_solution(14362522878635785008)
XLA Ops:
  1.3 29.6 %shard_map.50 = (f32[256,1024]{1,0:T(8,128)S(1)}, f32[256,1024]{1,0:T(8,128)S(1)}) custom-call(s32[1,1,1]{2,1,0:T(1,128)S(6)} %copy.5.pick_ref, s32[1,1,1,2]{3,2,1,0:T(1,128)} %off_hbm.1, f32[256,1024]{1,0:T(8,128)} %bitcast.3), custom_call_target="tpu_custom_call" | custom-call | tf_op jit(solution)/shard_map/pallas_call | solution.py:265
  30.8 1.3 %shard_map.51 = (f32[256,1024]{1,0:T(8,128)}, f32[256,1024]{1,0:T(8,128)}) custom-call(f32[256,1024]{1,0:T(8,128)S(1)} %get-tuple-element.6.next_in, f32[256,1024]{1,0:T(8,128)S(1)} %get-tuple-element.7.prev_in), custom_call_target="tpu_custom_call" | custom-call | tf_op jit(solution)/shard_map/pallas_call | solution.py:281

commit v4 on v3

--- a/solution.py
+++ b/solution.py
@@ -109,7 +109,7 @@
     yh[...], yl[...] = split(jnp.where(column < SPAN, tap_weights(step, 1.0, frac_y), -tap_weights(step, 2.0, frac_y)))
 
     def convert(r0, r1, c0, c1):
-        ph[r0:r1, c0:c1], plo[r0:r1, c0:c1] = split(pf[r0:r1, c0:c1])
+        ph[r0:r1, c0:c1], plo[r0:r1, c0:c1] = split(pf[r0:r1, c0:c1] - level)
 
     def compute(first, pair):
         for n, j in enumerate(pair):
@@ -149,6 +149,7 @@
         for i, (source, target, to) in enumerate(((LANE, LANE + TW, tx - 1), (TW, 0, tx + 1))))
 
     loads[0].wait()
+    level = jnp.mean(pf[64:72, LANE:2 * LANE])
     convert(64, 160, LANE, LANE + 512)
     compute(UPPER, INNER[0][:1])
     pl.semaphore_wait(bar, count([has_next, has_prev] + leads))

time: 32.4 us -> 32.5 us (level)
  no operation moved by 1% of the time
where the time goes in v4:
time: 32.5 us; the launch traced here: 32.3 us
  Pallas kernels  31 us (95%)
  between operations  1.28 us (4%)
    pallas_call x1, Pallas kernels, body(): pl.pallas_call(kernel, out_shape=[tile, tile], in_specs=[pl.BlockSpec(mem...  29.7 us
    pallas_call x1, Pallas kernels, body(): pl.pallas_call(flush, out_shape=[tile, tile], in_specs=[pl.BlockSpec(memo...  1.33 us

profile of v4, /device:TPU:7, one launch (start us, length us, event | category | flops | bytes accessed | tf_op | source)
XLA Modules:
  0.0 32.3 jit_solution(6957840817060118862)
XLA Ops:
  1.3 29.7 %shard_map.50 = (f32[256,1024]{1,0:T(8,128)S(1)}, f32[256,1024]{1,0:T(8,128)S(1)}) custom-call(s32[1,1,1]{2,1,0:T(1,128)S(6)} %copy.5.pick_ref, s32[1,1,1,2]{3,2,1,0:T(1,128)} %off_hbm.1, f32[256,1024]{1,0:T(8,128)} %bitcast.3), custom_call_target="tpu_custom_call" | custom-call | tf_op jit(solution)/shard_map/pallas_call | solution.py:266
  30.9 1.3 %shard_map.51 = (f32[256,1024]{1,0:T(8,128)}, f32[256,1024]{1,0:T(8,128)}) custom-call(f32[256,1024]{1,0:T(8,128)S(1)} %get-tuple-element.6.next_in, f32[256,1024]{1,0:T(8,128)S(1)} %get-tuple-element.7.prev_in), custom_call_target="tpu_custom_call" | custom-call | tf_op jit(solution)/shard_map/pallas_call | solution.py:282

commit v5 on v3

--- a/solution.py
+++ b/solution.py
@@ -51,7 +51,7 @@
     return dot(ah, bh) + dot(ah, bl) + dot(al, bh)
 
 
-def kernel(pick_ref, off_hbm, x_ref, next_ref, prev_ref, off_ref, pf, ph, plo, wh, wl, yh, yl, hh, hl, dog, bn, bp,
+def kernel(pick_ref, off_hbm, x_ref, next_ref, prev_ref, off_ref, pf, wh, wl, yh, yl, hh, hl, dog, bn, bp,
            load_sem, row_send, row_recv, col_send, col_recv, send_sem, recv_sem, ready):
     die, ty, tx = lax.axis_index("die"), lax.axis_index("ty"), lax.axis_index("tx")
     dies, tys, txs = lax.axis_size("die"), lax.axis_size("ty"), lax.axis_size("tx")
@@ -62,6 +62,18 @@
         def _(target=target):
             pl.semaphore_signal(bar, inc=1, device_id={"die": target}, device_id_type=MESH)
 
+    def load(i, first, rows, left, columns):
+        return pltpu.make_async_copy(x_ref.at[pl.ds(first, rows), pl.ds(left, columns)],
+                                     pf.at[pl.ds(PAD + first, rows), pl.ds(LANE + left, columns)], load_sem.at[i])
+
+    small = pltpu.make_async_copy(off_hbm, off_ref, load_sem.at[0])
+    loads = (load(1, 48, 96, 0, 512), load(2, 144, 64, 0, 512), load(3, 48, 160, 512, 512), load(4, 0, 96, 0, TW))
+    small.start()
+    for first in (48, 80, 112):
+        load(1, first, 32, 0, 512).start()
+    for copy in (loads[1], loads[2], load(4, 0, 48, 0, TW), load(4, 208, 48, 0, TW)):
+        copy.start()
+
     has_above, has_below, has_left, has_right = ty > 0, ty < tys - 1, tx > 0, tx < txs - 1
     count = lambda flags: sum(flag.astype(jnp.int32) for flag in flags)
 
@@ -79,16 +91,6 @@
         @pl.when(flag)
         def _(target=target):
             pl.semaphore_signal(bar, inc=1, device_id=target, device_id_type=MESH)
-
-    small = pltpu.make_async_copy(off_hbm, off_ref, load_sem.at[0])
-    small.start()
-    loads = []
-    for i, (first, rows, left, columns) in enumerate(((48, 96, 0, 512), (144, 64, 0, 512), (48, 160, 512, 512), (0, 48, 0, TW), (208, 48, 0, TW))):
-        copy = pltpu.make_async_copy(x_ref.at[pl.ds(first, rows), pl.ds(left, columns)],
-                                     pf.at[pl.ds(PAD + first, rows), pl.ds(LANE + left, columns)], load_sem.at[min(i + 1, 4)])
-        copy.start()
-        loads.append(copy)
-    edges = pltpu.make_async_copy(x_ref.at[pl.ds(0, 96)], pf.at[pl.ds(PAD, 96), pl.ds(LANE, TW)], load_sem.at[4])
 
     band = slice(LANE - PAD, 2 * LANE + PAD)
     for w in (wh, wl):
@@ -108,14 +110,12 @@
     step = jnp.where(column < SPAN, column, column - SPAN) - PAD - iota((ROWS, 2 * SPAN), 0) - row_off
     yh[...], yl[...] = split(jnp.where(column < SPAN, tap_weights(step, 1.0, frac_y), -tap_weights(step, 2.0, frac_y)))
 
-    def convert(r0, r1, c0, c1):
-        ph[r0:r1, c0:c1], plo[r0:r1, c0:c1] = split(pf[r0:r1, c0:c1])
-
     def compute(first, pair):
+        level = jnp.mean(pf[first + 40:first + 48, (pair[0] + 1) * LANE:(pair[0] + 2) * LANE], keepdims=True)
         for n, j in enumerate(pair):
-            lanes = slice(j * LANE, (j + 3) * LANE)
-            h = product(ph[first:first + SPAN, lanes], plo[first:first + SPAN, lanes], wh[...], wl[...])
-            high, low = split(h)
+            if pair == OUTER and n == 1:
+                level = jnp.mean(pf[first + 40:first + 48, (j + 1) * LANE:(j + 2) * LANE], keepdims=True)
+            high, low = split(product(*split(pf[first:first + SPAN, j * LANE:(j + 3) * LANE] - level), wh[...], wl[...]))
             for s in range(2):
                 where = (slice(s * SPAN, (s + 1) * SPAN), slice(n * LANE, (n + 1) * LANE))
                 hh[where], hl[where] = high[:, s * LANE:(s + 1) * LANE], low[:, s * LANE:(s + 1) * LANE]
@@ -149,7 +149,6 @@
         for i, (source, target, to) in enumerate(((LANE, LANE + TW, tx - 1), (TW, 0, tx + 1))))
 
     loads[0].wait()
-    convert(64, 160, LANE, LANE + 512)
     compute(UPPER, INNER[0][:1])
     pl.semaphore_wait(bar, count([has_next, has_prev] + leads))
     for (target, _, _, slot), flag in zip(sides, leads):
@@ -161,16 +160,14 @@
     compute(UPPER, INNER[0][1:])
     send(1)
     loads[1].wait()
-    convert(160, 224, LANE, LANE + 512)
     compute(LOWER, INNER[0])
     send(2)
     loads[2].wait()
-    edges.wait()
+    loads[3].wait()
     pl.when(leads[ABOVE])(to_above.start)
     pl.when(leads[BELOW])(to_below.start)
     pl.when(leads[LEFT])(to_left[0].start)
     pl.when(leads[RIGHT])(to_right[0].start)
-    convert(64, 224, LANE + 512, LANE + TW)
     for i, pair in enumerate(INNER[1:]):
         compute(UPPER, pair)
         compute(LOWER, pair)
@@ -192,8 +189,6 @@
     for i in (1, 2):
         pl.when(leads[LEFT])(to_left[i].start)
         pl.when(leads[RIGHT])(to_right[i].start)
-    convert(0, 64, LANE, LANE + TW)
-    convert(224, 288, LANE, LANE + TW)
     for i, first in enumerate((TOP, BOTTOM)):
         for pair in INNER:
             compute(first, pair)
@@ -214,8 +209,6 @@
 
     pl.when(has_right)(to_left[3].wait_recv)
     pl.when(has_left)(to_right[3].wait_recv)
-    convert(0, 288, 0, LANE)
-    convert(0, 288, LANE + TW, 2 * LANE + TW)
     for first in (TOP, UPPER, LOWER, BOTTOM):
         compute(first, OUTER)
     send(7)
@@ -269,7 +262,7 @@
         out_specs=[pl.BlockSpec(memory_space=pltpu.VMEM)] * 2,
         scratch_shapes=[
             pltpu.SMEM((1, 1, 1, 2), jnp.int32),
-            pltpu.VMEM((high, wide), F32), pltpu.VMEM((high, wide), BF16), pltpu.VMEM((high, wide), BF16),
+            pltpu.VMEM((high, wide), F32),
             pltpu.VMEM((3 * LANE, 2 * LANE), BF16), pltpu.VMEM((3 * LANE, 2 * LANE), BF16),
             pltpu.VMEM((ROWS, 2 * SPAN), BF16), pltpu.VMEM((ROWS, 2 * SPAN), BF16),
             pltpu.VMEM((2 * SPAN, 2 * LANE), BF16), pltpu.VMEM((2 * SPAN, 2 * LANE), BF16),

time: 32.4 us -> 32.6 us (level)
  no operation moved by 1% of the time
where the time goes in v5:
time: 32.6 us; the launch traced here: 32.3 us
  Pallas kernels  31 us (95%)
  between operations  1.28 us (4%)
    pallas_call x1, Pallas kernels, body(): pl.pallas_call(kernel, out_shape=[tile, tile], in_specs=[pl.BlockSpec(mem...  29.7 us
    pallas_call x1, Pallas kernels, body(): pl.pallas_call(flush, out_shape=[tile, tile], in_specs=[pl.BlockSpec(memo...  1.33 us

profile of v5, /device:TPU:7, one launch (start us, length us, event | category | flops | bytes accessed | tf_op | source)
XLA Modules:
  0.0 32.3 jit_solution(7984524002336730524)
XLA Ops:
  1.3 29.7 %shard_map.50 = (f32[256,1024]{1,0:T(8,128)S(1)}, f32[256,1024]{1,0:T(8,128)S(1)}) custom-call(s32[1,1,1]{2,1,0:T(1,128)S(6)} %copy.5.pick_ref, s32[1,1,1,2]{3,2,1,0:T(1,128)} %off_hbm.1, f32[256,1024]{1,0:T(8,128)} %bitcast.3), custom_call_target="tpu_custom_call" | custom-call | tf_op jit(solution)/shard_map/pallas_call | solution.py:258
  30.9 1.3 %shard_map.51 = (f32[256,1024]{1,0:T(8,128)}, f32[256,1024]{1,0:T(8,128)}) custom-call(f32[256,1024]{1,0:T(8,128)S(1)} %get-tuple-element.6.next_in, f32[256,1024]{1,0:T(8,128)S(1)} %get-tuple-element.7.prev_in), custom_call_target="tpu_custom_call" | custom-call | tf_op jit(solution)/shard_map/pallas_call | solution.py:274

commit v6 on v5

--- a/solution.py
+++ b/solution.py
@@ -22,7 +22,7 @@
 GROUPS = (((64, 64, 1, 1), (64, 64, 2, 1), (128, 64, 1, 2), (64, 128, 3, 2), (64, 128, 5, 2)),
           ((0, 64, 1, 6), (192, 64, 1, 6)),
           ((0, 256, 0, 1), (0, 256, 7, 1)))
-ARRIVALS = ((128, 768), (128, 768), (256, 256))
+ARRIVALS = ((6, 128), (6, 128), (2, 256))
 
 
 def start_rank(die, ty, tx):
@@ -67,11 +67,11 @@
                                      pf.at[pl.ds(PAD + first, rows), pl.ds(LANE + left, columns)], load_sem.at[i])
 
     small = pltpu.make_async_copy(off_hbm, off_ref, load_sem.at[0])
-    loads = (load(1, 48, 96, 0, 512), load(2, 144, 64, 0, 512), load(3, 48, 160, 512, 512), load(4, 0, 96, 0, TW))
+    loads = (load(1, 48, 96, 0, 512), load(2, 0, 208, 0, TW))
     small.start()
     for first in (48, 80, 112):
         load(1, first, 32, 0, 512).start()
-    for copy in (loads[1], loads[2], load(4, 0, 48, 0, TW), load(4, 208, 48, 0, TW)):
+    for copy in (load(2, 144, 64, 0, 512), load(2, 48, 160, 512, 512), load(2, 0, 48, 0, TW), load(2, 208, 48, 0, TW)):
         copy.start()
 
     has_above, has_below, has_left, has_right = ty > 0, ty < tys - 1, tx > 0, tx < txs - 1
@@ -122,14 +122,14 @@
         wide = slice(0, len(pair) * LANE)
         d = product(yh[...], yl[...], hh[:, wide], hl[:, wide])
         for n, j in enumerate(pair):
-            dog[first:first + ROWS, j * LANE:(j + 1) * LANE] = d[:, n * LANE:(n + 1) * LANE]
+            dog[j, first:first + ROWS, :] = d[:, n * LANE:(n + 1) * LANE]
 
     def transfer(k, group, where):
         target, landing = ((die - 1, bn), (die + 1, bp))[k]
         return pltpu.make_async_remote_copy(src_ref=dog.at[where], dst_ref=landing.at[where], send_sem=send_sem.at[k], recv_sem=recv_sem.at[k, group],
                                             device_id={"die": target}, device_id_type=MESH)
 
-    spots = [[(pl.ds(first, rows), pl.ds(left * LANE, blocks * LANE)) for first, rows, left, blocks in group] for group in GROUPS]
+    spots = [[(pl.ds(left, blocks), pl.ds(first, rows)) for first, rows, left, blocks in group] for group in GROUPS]
     pieces = [[transfer(k, g, where) for k in range(2)] for g, group in enumerate(spots) for where in group]
 
     def send(i):
@@ -162,8 +162,6 @@
     loads[1].wait()
     compute(LOWER, INNER[0])
     send(2)
-    loads[2].wait()
-    loads[3].wait()
     pl.when(leads[ABOVE])(to_above.start)
     pl.when(leads[BELOW])(to_below.start)
     pl.when(leads[LEFT])(to_left[0].start)
@@ -219,22 +217,26 @@
         def _(ref=ref):
             ref[...] = jnp.zeros((TH, TW), F32)
 
-    for g, (group, (rows, columns)) in enumerate(zip(spots, ARRIVALS)):
-        block = (pl.ds(0, rows), pl.ds(0, columns))
+    for g, (group, (blocks, rows)) in enumerate(zip(GROUPS, ARRIVALS)):
+        region = (pl.ds(0, blocks), pl.ds(0, rows))
 
         @pl.when(has_next)
-        def _(g=g, group=group, block=block):
-            transfer(0, g, block).wait_recv()
-            for where in group:
-                next_ref[where] = bn[where] - dog[where]
+        def _(g=g, group=group, region=region):
+            transfer(0, g, region).wait_recv()
+            for first, rows, left, blocks in group:
+                for j in range(left, left + blocks):
+                    where = (j, slice(first, first + rows))
+                    next_ref[first:first + rows, j * LANE:(j + 1) * LANE] = bn[where] - dog[where]
 
         @pl.when(has_prev)
-        def _(g=g, group=group, block=block):
-            transfer(1, g, block).wait_recv()
-            for where in group:
-                prev_ref[where] = dog[where] - bp[where]
-
-    tile = (pl.ds(0, TH), pl.ds(0, TW))
+        def _(g=g, group=group, region=region):
+            transfer(1, g, region).wait_recv()
+            for first, rows, left, blocks in group:
+                for j in range(left, left + blocks):
+                    where = (j, slice(first, first + rows))
+                    prev_ref[first:first + rows, j * LANE:(j + 1) * LANE] = dog[where] - bp[where]
+
+    tile = (pl.ds(0, TW // LANE), pl.ds(0, TH))
     pl.when(has_prev)(transfer(0, 0, tile).wait_send)
     pl.when(has_next)(transfer(1, 0, tile).wait_send)
     pl.when(has_above)(to_above.wait_send)
@@ -266,8 +268,8 @@
             pltpu.VMEM((3 * LANE, 2 * LANE), BF16), pltpu.VMEM((3 * LANE, 2 * LANE), BF16),
             pltpu.VMEM((ROWS, 2 * SPAN), BF16), pltpu.VMEM((ROWS, 2 * SPAN), BF16),
             pltpu.VMEM((2 * SPAN, 2 * LANE), BF16), pltpu.VMEM((2 * SPAN, 2 * LANE), BF16),
-            pltpu.VMEM((TH, TW), F32), pltpu.VMEM((TH, TW), F32), pltpu.VMEM((TH, TW), F32),
-            dma((5,)), dma((2,)), dma((2,)), dma((2,)), dma((2,)), dma((2,)), dma((2, 3)), pltpu.SemaphoreType.REGULAR((4,)),
+            *[pltpu.VMEM((TW // LANE, TH, LANE), F32)] * 3,
+            dma((3,)), dma((2,)), dma((2,)), dma((2,)), dma((2,)), dma((2,)), dma((2, 3)), pltpu.SemaphoreType.REGULAR((4,)),
         ],
         compiler_params=pltpu.CompilerParams(collective_id=0, has_side_effects=True, vmem_limit_bytes=32 * 1024 * 1024),
     )(shift_pick, *(pltpu.with_memory_space_constraint(x, pltpu.HBM) for x in (offsets, raster[0])))

time: 32.6 us -> 32.6 us (level)
  no operation moved by 1% of the time
where the time goes in v6:
time: 32.6 us; the launch traced here: 32.2 us
  Pallas kernels  31 us (95%)
  between operations  1.28 us (4%)
    pallas_call x1, Pallas kernels, body(): pl.pallas_call(kernel, out_shape=[tile, tile], in_specs=[pl.BlockSpec(mem...  29.6 us
    pallas_call x1, Pallas kernels, body(): pl.pallas_call(flush, out_shape=[tile, tile], in_specs=[pl.BlockSpec(memo...  1.33 us

profile of v6, /device:TPU:7, one launch (start us, length us, event | category | flops | bytes accessed | tf_op | source)
XLA Modules:
  0.0 32.2 jit_solution(16596369406174392936)
XLA Ops:
  1.3 29.6 %shard_map.50 = (f32[256,1024]{1,0:T(8,128)S(1)}, f32[256,1024]{1,0:T(8,128)S(1)}) custom-call(s32[1,1,1]{2,1,0:T(1,128)S(6)} %copy.5.pick_ref, s32[1,1,1,2]{3,2,1,0:T(1,128)} %off_hbm.1, f32[256,1024]{1,0:T(8,128)} %bitcast.3), custom_call_target="tpu_custom_call" | custom-call | tf_op jit(solution)/shard_map/pallas_call | solution.py:260
  30.9 1.3 %shard_map.51 = (f32[256,1024]{1,0:T(8,128)}, f32[256,1024]{1,0:T(8,128)}) custom-call(f32[256,1024]{1,0:T(8,128)S(1)} %get-tuple-element.6.next_in, f32[256,1024]{1,0:T(8,128)S(1)} %get-tuple-element.7.prev_in), custom_call_target="tpu_custom_call" | custom-call | tf_op jit(solution)/shard_map/pallas_call | solution.py:276

commit v7 on v5

--- a/solution.py
+++ b/solution.py
@@ -211,8 +211,6 @@
     pl.when(has_left)(to_right[3].wait_recv)
     for first in (TOP, UPPER, LOWER, BOTTOM):
         compute(first, OUTER)
-    send(7)
-    send(8)
 
     for there, ref in ((has_next, next_ref), (has_prev, prev_ref)):
         @pl.when(jnp.logical_not(there))
@@ -233,6 +231,10 @@
             transfer(1, g, block).wait_recv()
             for where in group:
                 prev_ref[where] = dog[where] - bp[where]
+
+        if g == 0:
+            send(7)
+            send(8)
 
     tile = (pl.ds(0, TH), pl.ds(0, TW))
     pl.when(has_prev)(transfer(0, 0, tile).wait_send)

time: 32.6 us -> 32.5 us (level)
  no operation moved by 1% of the time
where the time goes in v7:
time: 32.5 us; the launch traced here: 32.3 us
  Pallas kernels  31 us (95%)
  between operations  1.28 us (4%)
    pallas_call x1, Pallas kernels, body(): pl.pallas_call(kernel, out_shape=[tile, tile], in_specs=[pl.BlockSpec(mem...  29.7 us
    pallas_call x1, Pallas kernels, body(): pl.pallas_call(flush, out_shape=[tile, tile], in_specs=[pl.BlockSpec(memo...  1.33 us

profile of v7, /device:TPU:7, one launch (start us, length us, event | category | flops | bytes accessed | tf_op | source)
XLA Modules:
  0.0 32.3 jit_solution(1642339007870790272)
XLA Ops:
  1.3 29.7 %shard_map.50 = (f32[256,1024]{1,0:T(8,128)S(1)}, f32[256,1024]{1,0:T(8,128)S(1)}) custom-call(s32[1,1,1]{2,1,0:T(1,128)S(6)} %copy.5.pick_ref, s32[1,1,1,2]{3,2,1,0:T(1,128)} %off_hbm.1, f32[256,1024]{1,0:T(8,128)} %bitcast.3), custom_call_target="tpu_custom_call" | custom-call | tf_op jit(solution)/shard_map/pallas_call | solution.py:260
  30.9 1.3 %shard_map.51 = (f32[256,1024]{1,0:T(8,128)}, f32[256,1024]{1,0:T(8,128)}) custom-call(f32[256,1024]{1,0:T(8,128)S(1)} %get-tuple-element.6.next_in, f32[256,1024]{1,0:T(8,128)S(1)} %get-tuple-element.7.prev_in), custom_call_target="tpu_custom_call" | custom-call | tf_op jit(solution)/shard_map/pallas_call | solution.py:276
